TPU v7x, 256 devices: a whole 4x4x8 slice. The times are simulated.
256 devices in a mesh: src: 8 (over y, core), tp: 16 (over x, z_hi), row: 2 (over z_lo).
Axes of the slice: x: 4, y: 4, z: 8 (z_hi: 4, z_lo: 2; z = z_hi * 2 + z_lo), core: 2. Of those that a mesh axis runs over, the one named last changes fastest.
Arguments:
- tokens: bfloat16 [8, 256, 8192], P('src', 'tp', 'row'), may hold values from -6 to 6
- coefficients: float32 [8, 8], replicated, may hold values from -2 to 2
- gate_weights: bfloat16 [8, 8192, 4096], P('src', 'row', 'tp'), may hold values from -0.0625 to 0.0625
- up_weights: bfloat16 [8, 8192, 4096], P('src', 'row', 'tp'), may hold values from -0.0625 to 0.0625
Outputs:
- hidden: bfloat16 [8, 256, 4096], P('src', 'row', 'tp')
All inputs are finite; a program needn't handle non-finite values.
Results may differ from a plain program's by a relative error of at most 0.0013.
Values may be sent and summed in bfloat16 or wider, within the bound.
A program may use at most 64 MiB of HBM per device.

v0:
```python
import jax
import jax.numpy as jnp
from jax import lax
from jax.sharding import PartitionSpec as P


def split_up(array, dim, devices):
    shape = array.shape
    tiles = array.reshape(*shape[:dim], devices, shape[dim] // devices, *shape[dim + 1 :])
    return jnp.moveaxis(tiles, dim, 0)


def sent_and_summed(array, axis, dim):
    tiles = split_up(array, dim, lax.axis_size(axis))
    arrived = lax.all_to_all(tiles, axis, split_axis=0, concat_axis=0, tiled=True)
    return arrived.sum(axis=0)


def shards(tokens, coefficients, gate_weights, up_weights):
    local_rows = tokens.shape[1]
    half_width = tokens.shape[2]
    candidates = coefficients.shape[0]
    sources = coefficients.shape[1]
    per_candidate = local_rows * lax.axis_size("tp")
    out_rows = per_candidate // lax.axis_size("row")
    own_source = lax.axis_index("src")
    picked = (jnp.arange(sources, dtype=jnp.int32) == own_source).astype(jnp.float32)
    own_factors = jnp.sum(coefficients * picked[None, :], axis=1)
    gate_local = gate_weights[0]
    up_local = up_weights[0]
    hidden_width = gate_local.shape[1]
    flat_tokens = tokens.reshape(local_rows, half_width)
    row_block = lax.all_gather(flat_tokens, ("src", "tp"), axis=0, tiled=True)
    row_count = row_block.shape[0]
    owner_ids = jnp.arange(row_count, dtype=jnp.int32) // per_candidate
    one_hot = (owner_ids[:, None] == jnp.arange(candidates, dtype=jnp.int32)[None, :]).astype(
        jnp.float32
    )
    factor = jnp.sum(one_hot * own_factors[None, :], axis=1)[:, None]
    gate_part = jnp.dot(row_block, gate_local, preferred_element_type=jnp.float32)
    up_part = jnp.dot(row_block, up_local, preferred_element_type=jnp.float32)
    collected = jnp.concatenate((gate_part, up_part), axis=1) * factor
    summed = sent_and_summed(collected, ("src", "row"), 0)
    hidden = (jax.nn.silu(summed[:, :hidden_width]) * summed[:, hidden_width:]).astype(jnp.bfloat16)
    return hidden.reshape(1, out_rows, hidden_width)


def solution(mesh):
    return jax.shard_map(
        shards,
        mesh=mesh,
        in_specs=(P("src", "tp", "row"), P(), P("src", "row", "tp"), P("src", "row", "tp")),
        out_specs=P("src", "row", "tp"),
        check_vma=False,
    )
```

profile of v0, /device:TPU:1, one launch (start us, length us, event | category | flops | bytes accessed | tf_op | source)
XLA Modules:
  0.0 212.2 jit_solution(2710372214216165005)
XLA Ops:
  6.5 0.0 copy-start
  6.5 0.0 all-gather.3.cloned.1.call-start
  6.5 0.7 all-gather.3.cloned.1.call-update
  7.3 0.8 multiply_reduce_fusion
  8.1 0.1 select_reduce_fusion
  8.2 123.5 %all-gather.3.cloned.1.call-done = bf16[1,2048,4096]{2,1,0:T(8,128)(2,1)} async-done(((bf16[1,16,4096]{2,1,0:T(8,128)(2,1)}), bf16[1,2048,4096]{2,1,0:T(8,128)(2,1)}) %all-gather.3.cloned.1.call-update) | async-done | bytes 16777232 | tf_op jit(solution)/shard_map/all_gather | solution.py:33
  131.7 0.0 copy-done
  131.7 0.0 copy-start.1
  131.7 0.0 copy-start.2
  131.7 8.3 %fusion = f32[16,128,256]{2,1,0:T(8,128)S(1)} fusion(bf16[16,128,4096]{2,1,0:T(8,128)(2,1)} %bitcast.15, bf16[1,4096,256]{2,1,0:T(8,128)(2,1)S(1)} %copy-done), kind=kOutput, calls=%fused_computation.1 | convolution fusion | flops 4294967296 | bytes 20971520 | tf_op jit(solution)/shard_map/dot_general | solution.py:41
  140.0 2.3 %copy-done.1 = bf16[1,2048,4096]{2,1,0:T(8,128)(2,1)S(1)} copy-done((bf16[1,2048,4096]{2,1,0:T(8,128)(2,1)S(1)}, bf16[1,2048,4096]{2,1,0:T(8,128)(2,1)}, u32[]{:S(2)}) %copy-start.1) | copy-done | bytes 16777240
  142.3 0.6 copy-done.2
  142.9 4.9 %fusion.2 = f32[16,128,256]{2,1,0:T(8,128)S(1)} fusion(bf16[16,128,4096]{2,1,0:T(8,128)(2,1)S(1)} %bitcast.16, bf16[1,4096,256]{2,1,0:T(8,128)(2,1)S(1)} %copy-done.2), kind=kOutput, calls=%fused_computation.3 | convolution fusion | flops 4294967296 | bytes 20971520 | tf_op jit(solution)/shard_map/dot_general | solution.py:40
  147.8 0.4 maximum_multiply_fusion
  148.2 53.9 %all_to_all.5 = f32[16,128,512]{2,1,0:T(8,128)} all-to-all(f32[16,128,512]{2,1,0:T(8,128)S(1)} %maximum_multiply_fusion), channel_id=1, replica_groups=mesh['src'=8,'tp'=16,'row'=2] {'src','row'}, dimensions={0} | all-to-all | bytes 8388608 | tf_op jit(solution)/shard_map/all_to_all | solution.py:15
  202.0 2.6 %reduce_sum.29 = f32[128,512]{1,0:T(8,128)S(1)} reduce(f32[16,128,512]{2,1,0:T(8,128)} %all_to_all.5, f32[]{:T(128)} %constant.28.clone.1), dimensions={0}, to_apply=%region_2.3 | reduce | flops 983040 | bytes 4456452 | tf_op jit(solution)/shard_map/reduce_sum | solution.py:16
  204.7 0.7 fusion.5
  (2 shorter events, 0.0 us)
Async XLA Ops:
  6.5 125.2 %copy-start = (bf16[1,4096,256]{2,1,0:T(8,128)(2,1)S(1)}, bf16[1,4096,256]{2,1,0:T(8,128)(2,1)}, u32[]{:S(2)}) copy-start(bf16[1,4096,256]{2,1,0:T(8,128)(2,1)} %param.7) | copy-start | bytes 6291460
  6.5 125.2 %all-gather.3.cloned.1.call-start = ((), (), s32[]{:S(2)}) async-start(), calls=%async_computation.1 | async-start | bytes 16908288 | tf_op jit(solution)/shard_map/all_gather | solution.py:33
  131.7 10.5 %copy-start.1 = (bf16[1,2048,4096]{2,1,0:T(8,128)(2,1)S(1)}, bf16[1,2048,4096]{2,1,0:T(8,128)(2,1)}, u32[]{:S(2)}) copy-start(bf16[1,2048,4096]{2,1,0:T(8,128)(2,1)} %all-gather.3.cloned.1.call-done) | copy-start | bytes 50331652
  131.7 11.1 %copy-start.2 = (bf16[1,4096,256]{2,1,0:T(8,128)(2,1)S(1)}, bf16[1,4096,256]{2,1,0:T(8,128)(2,1)}, u32[]{:S(2)}) copy-start(bf16[1,4096,256]{2,1,0:T(8,128)(2,1)} %param.6) | copy-start | bytes 6291460
Sparse Core Ops, SparseCore 0:
  10.9 120.7 all-gather.2
where the time goes:
time: 212 us
  waiting for transfers between devices  124 us (58%)
  blocking collectives  53.9 us (25%)
  between operations  13.4 us (6%)
  matrix products  13.2 us (6%)
  other arithmetic  4.6 us (2%)
  local copies, waits for them, and re-layouts  2.86 us (1%)
    all_gather x1, waiting for transfers between devices, shards(): row_block = lax.all_gather(flat_tokens, ('src', 'tp'), axis=0, tiled=True)  124 us
    all_to_all x1, blocking collectives, sent_and_summed(): lax.all_to_all(tiles, axis, split_axis=0, concat_axis=0, tiled=True)  53.9 us
    dot_general x1, matrix products, shards(): up_part = jnp.dot(row_block, up_local, preferred_element_type=jnp.float32)  8.28 us
    dot_general x1, matrix products, shards(): jnp.dot(row_block, gate_local, preferred_element_type=jnp.float32)  4.9 us
  transfers between devices with their start and end apart: 1, of which 1 were waited for; matrix products, arithmetic and copies ran while one was open for 0% of the time, Pallas kernels for 0%

commit v1 on v0

--- a/solution.py
+++ b/solution.py
@@ -30,7 +30,12 @@
     up_local = up_weights[0]
     hidden_width = gate_local.shape[1]
     flat_tokens = tokens.reshape(local_rows, half_width)
-    row_block = lax.all_gather(flat_tokens, ("src", "tp"), axis=0, tiled=True)
+    row_block = jnp.concatenate(
+        lax.all_to_all(
+            jnp.stack([flat_tokens] * lax.axis_size(("src", "tp"))), ("src", "tp"), 0, 0
+        ),
+        axis=0,
+    )
     row_count = row_block.shape[0]
     owner_ids = jnp.arange(row_count, dtype=jnp.int32) // per_candidate
     one_hot = (owner_ids[:, None] == jnp.arange(candidates, dtype=jnp.int32)[None, :]).astype(

time: 212 us -> 474 us (2.24); the launches traced: 212 us -> 468 us
  waiting for transfers between devices: 124 us -> 370 us
  starting transfers between devices: 0.01 us -> 17 us
  between operations: 13.4 us -> 0.08 us
    all_to_all x0 -> x1, waiting for transfers between devices: none -> 370 us  [shards(): lax.all_to_all(jnp.stack([flat_tokens] * lax.axis_size(('src', 'tp'))), (...]
    all_gather x1 -> x0, waiting for transfers between devices: 124 us -> none  [shards(): row_block = lax.all_gather(flat_tokens, ('src', 'tp'), axis=0, tiled=True)]
    all_to_all x0 -> x1, starting transfers between devices: none -> 17 us  [shards(): lax.all_to_all(jnp.stack([flat_tokens] * lax.axis_size(('src', 'tp'))), (...]
    another operation x0 -> x1, local copies, waits for them, and re-layouts: none -> 6.86 us  [shards(): jnp.stack([flat_tokens] * lax.axis_size(('src', 'tp')))]
where the time goes in v1:
time: 474 us; the launch traced here: 468 us
  waiting for transfers between devices  370 us (78%)
  blocking collectives  53.4 us (11%)
  starting transfers between devices  17 us (4%)
  matrix products  16.4 us (3%)
  local copies, waits for them, and re-layouts  6.88 us (1%)
    all_to_all x1, waiting for transfers between devices, shards(): lax.all_to_all(jnp.stack([flat_tokens] * lax.axis_size(('src', 'tp'))), (...  370 us
    all_to_all x1, blocking collectives, sent_and_summed(): lax.all_to_all(tiles, axis, split_axis=0, concat_axis=0, tiled=True)  53.4 us
    all_to_all x1, starting transfers between devices, shards(): lax.all_to_all(jnp.stack([flat_tokens] * lax.axis_size(('src', 'tp'))), (...  17 us
  transfers between devices with their start and end apart: 1, of which 1 were waited for; matrix products, arithmetic and copies ran while one was open for 0% of the time, Pallas kernels for 0%

profile of v1, /device:TPU:1, one launch (start us, length us, event | category | flops | bytes accessed | tf_op | source)
XLA Modules:
  0.0 467.7 jit_solution(11336651642070040880)
XLA Ops:
  0.0 0.0 copy-start
  0.0 6.9 %stack.3 = bf16[128,16,4096]{2,1,0:T(8,128)(2,1)} broadcast(bf16[16,4096]{1,0:T(8,128)(2,1)} %bitcast.15), dimensions={1,2} | broadcast | bytes 16908288 | tf_op jit(solution)/shard_map/stack | solution.py:35
  6.9 0.0 copy-start.1
  6.9 17.0 %all-to-all-start = ((bf16[128,16,4096]{2,1,0:T(8,128)(2,1)}), bf16[128,16,4096]{2,1,0:T(8,128)(2,1)}, u32[]{:S(2)}, u32[]{:S(2)}) async-start(bf16[128,16,4096]{2,1,0:T(8,128)(2,1)} %stack.3), calls=%async_computation | async-start | bytes 33554432 | tf_op jit(solution)/shard_map/all_to_all | solution.py:34
  23.9 0.0 copy-done.1
  23.9 0.1 multiply_reduce_fusion
  24.0 0.1 select_reduce_fusion
  24.1 370.1 %all-to-all-done = bf16[128,16,4096]{2,1,0:T(8,128)(2,1)} async-done(((bf16[128,16,4096]{2,1,0:T(8,128)(2,1)}), bf16[128,16,4096]{2,1,0:T(8,128)(2,1)}, u32[]{:S(2)}, u32[]{:S(2)}) %all-to-all-start) | async-done | bytes 16777248 | tf_op jit(solution)/shard_map/all_to_all | solution.py:34
  394.2 0.0 copy-done
  394.2 0.0 copy-start.2
  394.2 8.3 %fusion = f32[16,128,256]{2,1,0:T(8,128)S(1)} fusion(bf16[16,128,4096]{2,1,0:T(8,128)(2,1)} %bitcast.1, bf16[1,4096,256]{2,1,0:T(8,128)(2,1)S(1)} %copy-done), kind=kOutput, calls=%fused_computation.1 | convolution fusion | flops 4294967296 | bytes 20971520 | tf_op jit(solution)/shard_map/dot_general | solution.py:46
  402.5 0.0 copy-done.2
  402.5 8.2 %fusion.2 = f32[16,128,256]{2,1,0:T(8,128)S(1)} fusion(bf16[16,128,4096]{2,1,0:T(8,128)(2,1)} %bitcast.1, bf16[1,4096,256]{2,1,0:T(8,128)(2,1)S(1)} %copy-done.2), kind=kOutput, calls=%fused_computation.3 | convolution fusion | flops 4294967296 | bytes 20971520 | tf_op jit(solution)/shard_map/dot_general | solution.py:45
  410.6 0.4 maximum_multiply_fusion
  411.0 53.4 %all_to_all.10 = f32[16,128,512]{2,1,0:T(8,128)} all-to-all(f32[16,128,512]{2,1,0:T(8,128)S(1)} %maximum_multiply_fusion), channel_id=1, replica_groups=mesh['src'=8,'tp'=16,'row'=2] {'src','row'}, dimensions={0} | all-to-all | bytes 8388608 | tf_op jit(solution)/shard_map/all_to_all | solution.py:15
  464.4 2.6 reduce_sum.29
  467.1 0.7 fusion.5
  (2 shorter events, 0.0 us)
Async XLA Ops:
  0.0 394.2 %copy-start = (bf16[1,4096,256]{2,1,0:T(8,128)(2,1)S(1)}, bf16[1,4096,256]{2,1,0:T(8,128)(2,1)}, u32[]{:S(2)}) copy-start(bf16[1,4096,256]{2,1,0:T(8,128)(2,1)} %param.7) | copy-start | bytes 6291460
  6.9 17.0 %copy-start.1 = (f32[8,8]{1,0:T(8,128)S(1)}, f32[8,8]{1,0:T(8,128)}, u32[]{:S(2)}) copy-start(f32[8,8]{1,0:T(8,128)} %param.5) | copy-start | bytes 772
  6.9 387.3 %all-to-all-start = ((bf16[128,16,4096]{2,1,0:T(8,128)(2,1)}), bf16[128,16,4096]{2,1,0:T(8,128)(2,1)}, u32[]{:S(2)}, u32[]{:S(2)}) async-start(bf16[128,16,4096]{2,1,0:T(8,128)(2,1)} %stack.3), calls=%async_computation | async-start | bytes 33554432 | tf_op jit(solution)/shard_map/all_to_all | solution.py:34
  394.2 8.3 %copy-start.2 = (bf16[1,4096,256]{2,1,0:T(8,128)(2,1)S(1)}, bf16[1,4096,256]{2,1,0:T(8,128)(2,1)}, u32[]{:S(2)}) copy-start(bf16[1,4096,256]{2,1,0:T(8,128)(2,1)} %param.6) | copy-start | bytes 6291460
